TPU v7x, 256 devices: a whole 4x4x8 slice. The times are simulated.
256 devices in a mesh: dom: 64 (over x, z, y_hi), head: 4 (over y_lo, core).
Axes of the slice: x: 4, y: 4 (y_hi: 2, y_lo: 2; y = y_hi * 2 + y_lo), z: 8, core: 2. Of those that a mesh axis runs over, the one named last changes fastest.
Arguments:
- vertex_embeddings: bfloat16 [32768, 512], P(('dom', 'head')), may hold values from -6 to 6
- adjacent_group_bank_ids: int32 [64, 4, 12], P('dom', 'head'), may hold values from -1 to 15, as said below
- coupling_strength_panels: bfloat16 [16, 128, 128], replicated, may hold values from -0.3125 to 0.3125
- asking_projector: bfloat16 [512, 512], replicated, may hold values from -0.25 to 0.25
- lookup_projector: bfloat16 [512, 512], replicated, may hold values from -0.25 to 0.25
- content_projector: bfloat16 [512, 512], replicated, may hold values from -0.25 to 0.25
- final_projector: bfloat16 [512, 512], replicated, may hold values from -0.25 to 0.25
- passing_inner_coefficients: bfloat16 [512, 1024], replicated, may hold values from -0.25 to 0.25
- passing_outer_coefficients: bfloat16 [1024, 512], replicated, may hold values from -0.1875 to 0.1875
- softness_per_subspace: float32 [8], replicated, may hold values from 0.5 to 2
- mixing_layer_gain: float32 [512], replicated, may hold values from 0.5 to 1.5
Outputs:
- result: bfloat16 [32768, 512], P(('dom', 'head'))
Inputs may be any that keep to these rules, and one draw needn't show every extreme that they name: `adjacent_group_bank_ids`: -1 marks a block without edges. The entry of a block for itself is never -1, nor is at least one entry for each neighbouring partition.
All inputs are finite; a program needn't handle non-finite values.
Results may differ from a plain program's by a relative error of at most 0.0054.
Values may be sent and summed in bfloat16 or wider, within the bound.
A program may use at most 64 MiB of HBM per device.

v0:
```python
import math
import jax
import jax.numpy as jnp
from jax import lax
from jax.sharding import Mesh
from jax.sharding import PartitionSpec as P

NUM_SUBSPACES = 8
SUBSPACE_WIDTH = 64
KEY_BLOCK = 2048
norm_eps = 1e-06
ROW = "x"
COLUMN = "z"
PAIR = "yhi"
DOM = (ROW, COLUMN, PAIR)
GROUP = (PAIR, "head")


def extended(shard, width):
    devices = lax.axis_size(ROW) * lax.axis_size(COLUMN) * lax.axis_size(PAIR)
    length = shard.shape[0]
    up = [(i, (i + 1) % devices) for i in range(devices - 1)]
    down = [(j, i) for i, j in up]
    last = lax.slice_in_dim(shard, length - width, length, axis=0)
    first = lax.slice_in_dim(shard, 0, width, axis=0)
    before = lax.ppermute(last, DOM, up)
    after = lax.ppermute(first, DOM, down)
    return jnp.concatenate([before, shard, after], axis=0)


def head_norm(projected, scales):
    rows = projected.shape[0]
    grouped = projected.reshape(rows, -1, SUBSPACE_WIDTH)
    mean_square = jnp.mean(grouped * grouped, axis=-1, keepdims=True)
    scaled = grouped * lax.rsqrt(mean_square + norm_eps)
    if scales is not None:
        scaled = scaled * scales[None, :, None]
    return scaled.reshape(rows, -1).astype(jnp.bfloat16)


def shards(
    vertex_embeddings,
    adjacent_group_bank_ids,
    coupling_strength_panels,
    asking_projector,
    lookup_projector,
    content_projector,
    final_projector,
    passing_inner_coefficients,
    passing_outer_coefficients,
    softness_per_subspace,
    mixing_layer_gain,
):
    block_len = vertex_embeddings.shape[0]
    group_size = lax.axis_size("head")
    pair_size = lax.axis_size(PAIR)
    members = group_size * pair_size
    slot_ids = adjacent_group_bank_ids.reshape(-1)
    halo_rows = extended(vertex_embeddings, block_len)
    me = lax.axis_index("head")
    gathered = [halo_rows]
    for shift in range(1, group_size):
        pairs = [(i, (i + shift) % group_size) for i in range(group_size)]
        gathered.append(lax.ppermute(halo_rows, "head", pairs))
    stacked = jnp.stack(gathered)
    order = (me - jnp.arange(group_size)) % group_size
    nearby = jnp.zeros_like(stacked).at[order].set(stacked).reshape(-1, halo_rows.shape[1])
    slot_order = slot_ids.reshape(3, group_size).T.reshape(-1)
    asking_vector_multiplier = softness_per_subspace / math.sqrt(SUBSPACE_WIDTH)
    queries = head_norm(
        jnp.dot(vertex_embeddings, asking_projector, preferred_element_type=jnp.float32),
        asking_vector_multiplier,
    )
    keys_all = head_norm(
        jnp.dot(vertex_embeddings, lookup_projector, preferred_element_type=jnp.float32), None
    )
    values_all = jnp.dot(
        vertex_embeddings, content_projector, preferred_element_type=jnp.float32
    ).astype(jnp.bfloat16)
    head_of = [j % group_size * pair_size + j // group_size for j in range(members)]
    member_of = [head_of.index(h) for h in range(NUM_SUBSPACES)]
    packed = jnp.stack(
        [
            t.reshape(block_len, NUM_SUBSPACES, SUBSPACE_WIDTH)
            for t in (queries, keys_all, values_all)
        ],
        axis=2,
    )[:, jnp.array(head_of)]
    packed = packed.reshape(block_len, -1)
    mine = lax.all_to_all(packed, GROUP, split_axis=1, concat_axis=0, tiled=True)
    query_rows = mine.shape[0]
    head_queries = mine[:, :SUBSPACE_WIDTH]
    key_values = mine[:, SUBSPACE_WIDTH:]
    selected = jnp.take(coupling_strength_panels, jnp.maximum(slot_order, 0), axis=0)
    selected = jnp.where((slot_order >= 0)[:, None, None], selected, jnp.zeros_like(selected))
    wide_tiles = jnp.transpose(selected, (1, 0, 2)).reshape(block_len, -1)
    aggregate = jnp.dot(wide_tiles, nearby, preferred_element_type=jnp.float32).astype(jnp.bfloat16)
    hidden = jax.nn.gelu(
        jnp.dot(aggregate, passing_inner_coefficients, preferred_element_type=jnp.float32)
    ).astype(jnp.bfloat16)
    local_term = jnp.dot(hidden, passing_outer_coefficients, preferred_element_type=jnp.float32)
    local_term, head_queries = lax.optimization_barrier((local_term, head_queries))
    kv_in = lax.all_gather(key_values, (ROW, COLUMN), axis=0, tiled=True)
    key_count = kv_in.shape[0]
    block_step = min(KEY_BLOCK, key_count)
    ones = jnp.ones((block_step, SUBSPACE_WIDTH), jnp.bfloat16)

    def accumulate(turn_index, totals):
        block = lax.dynamic_slice_in_dim(kv_in, turn_index * block_step, block_step, 0)
        scores = jnp.einsum(
            "qd,kd->qk", head_queries, block[:, :SUBSPACE_WIDTH], preferred_element_type=jnp.float32
        )
        weights = jnp.exp(scores).astype(jnp.bfloat16)
        widened = jnp.concatenate([block[:, SUBSPACE_WIDTH:], ones], axis=1)
        return totals + jnp.dot(weights, widened, preferred_element_type=jnp.float32)

    totals = lax.fori_loop(
        0,
        key_count // block_step,
        accumulate,
        jnp.zeros((query_rows, 2 * SUBSPACE_WIDTH), jnp.float32),
    )
    merged = (totals[:, :SUBSPACE_WIDTH] / totals[:, SUBSPACE_WIDTH : SUBSPACE_WIDTH + 1]).astype(
        jnp.bfloat16
    )
    back = lax.all_to_all(merged, GROUP, split_axis=0, concat_axis=1, tiled=True)
    node_heads = back.reshape(block_len, members, SUBSPACE_WIDTH)[:, jnp.array(member_of)]
    node_heads = node_heads.reshape(block_len, -1)
    attended = jnp.dot(node_heads, final_projector, preferred_element_type=jnp.float32)
    normed = (
        attended
        * lax.rsqrt(jnp.mean(attended * attended, axis=-1, keepdims=True) + norm_eps)
        * mixing_layer_gain
    )
    return (vertex_embeddings.astype(jnp.float32) + local_term + normed).astype(jnp.bfloat16)


def solution(mesh):
    n_dom, n_head = (mesh.shape["dom"], mesh.shape["head"])
    fine = Mesh(mesh.devices.reshape(n_dom // 16, 8, 2, n_head), (ROW, COLUMN, PAIR, "head"))
    in_specs = (
        P((ROW, COLUMN, PAIR, "head"), None),
        P(DOM, "head", None),
        P(),
        P(),
        P(),
        P(),
        P(),
        P(),
        P(),
        P(),
        P(),
    )
    out_specs = P((ROW, COLUMN, PAIR, "head"), None)
    return jax.shard_map(shards, mesh=fine, in_specs=in_specs, out_specs=out_specs, check_vma=False)
```

profile of v0, /device:TPU:1, one launch (start us, length us, event | category | flops | bytes accessed | tf_op | source)
XLA Modules:
  0.0 226.7 jit_solution(1230595181593717141)
XLA Ops:
  6.5 0.8 maximum_reduce_fusion
  7.6 1.4 fusion.22
  11.2 0.6 gather_fusion.1
  11.8 13.9 %all_to_all.35 = bf16[128,8,192]{0,2,1:T(8,128)(2,1)S(1)} all-to-all(bf16[128,8,192]{0,2,1:T(8,128)(2,1)S(1)} %bitcast.63), channel_id=1, replica_groups=mesh['x'=4,'z'=8,'yhi'=2,'head'=4] {'yhi','head'}, dimensions={1} | all-to-all | bytes 786432 | tf_op jit(solution)/shard_map/all_to_all | solution.py:90
  25.7 0.8 slice.39
  26.5 2.5 %collective-permute-start = (bf16[128,512]{1,0:T(8,128)(2,1)S(1)}, bf16[128,512]{1,0:T(8,128)(2,1)S(1)}, u32[]{:S(2)}, u32[]{:S(2)}) collective-permute-start(bf16[128,512]{1,0:T(8,128)(2,1)S(1)} %copy-done.1), channel_id=1, source_target_pairs={{0,4},{4,8},{8,12},{12,16},{16,20},{20,24},{24,28},{28,32},{32,36}... | collective-permute-start | bytes 393224 | tf_op jit(solution)/shard_map/ppermute | solution.py:26
  29.0 1.3 collective-permute-start.1
  30.3 0.6 collective-permute-done
  31.0 6.4 %collective-permute-done.1 = bf16[128,512]{1,0:T(8,128)(2,1)S(1)} collective-permute-done((bf16[128,512]{1,0:T(8,128)(2,1)S(1)}, bf16[128,512]{1,0:T(8,128)(2,1)S(1)}, u32[]{:S(2)}, u32[]{:S(2)}) %collective-permute-start.1) | collective-permute-done | bytes 131104 | tf_op jit(solution)/shard_map/ppermute | solution.py:27
  37.4 2.0 collective-permute-start.2
  39.4 1.2 collective-permute-start.3
  41.2 1.7 gather_fusion
  43.0 1.0 copy.69
  44.0 3.7 %collective-permute-done.2 = bf16[384,512]{1,0:T(8,128)(2,1)} collective-permute-done((bf16[384,512]{1,0:T(8,128)(2,1)S(1)}, bf16[384,512]{1,0:T(8,128)(2,1)}, u32[]{:S(2)}, u32[]{:S(2)}) %collective-permute-start.2) | collective-permute-done | bytes 393248 | tf_op jit(solution)/shard_map/ppermute | solution.py:64
  47.7 10.4 %collective-permute-done.3 = bf16[384,512]{1,0:T(8,128)(2,1)} collective-permute-done((bf16[384,512]{1,0:T(8,128)(2,1)S(1)}, bf16[384,512]{1,0:T(8,128)(2,1)}, u32[]{:S(2)}, u32[]{:S(2)}) %collective-permute-start.3) | collective-permute-done | bytes 393248 | tf_op jit(solution)/shard_map/ppermute | solution.py:64
  58.1 0.6 collective-permute-done.4
  58.8 1.6 pad_maximum_fusion
  60.3 1.3 broadcast_in_dim.47
  61.7 4.7 %scatter_fusion = bf16[4,384,512]{2,1,0:T(8,128)(2,1)} fusion(bf16[4,384,512]{2,1,0:T(8,128)(2,1)} %broadcast_in_dim.47, s32[4]{0:T(128)S(1)} %fusion.20, bf16[4,384,512]{2,1,0:T(8,128)(2,1)S(1)} %pad_maximum_fusion), kind=kCustom, calls=%fused_computation.3 | custom fusion | bytes 4718608 | tf_op jit(solution)/shard_map/scatter | solution.py:67
  66.4 2.3 %fusion.16 = bf16[128,1024]{1,0:T(8,128)(2,1)S(1)} fusion(bf16[512,1024]{1,0:T(8,128)(2,1)S(1)} %copy-done, bf16[128,1536]{0,1:T(8,128)(2,1)} %bitcast.72, bf16[1536,512]{1,0:T(8,128)(2,1)} %bitcast.62), kind=kOutput, calls=%fused_computation.23 | convolution fusion | flops 336789504 | bytes 3276800 | tf_op jit(solution)/shard_map/dot_general | solution.py:99
  68.7 0.3 fusion.23
  69.0 0.6 slice-done
  69.8 56.1 %all-gather.2.cloned.1.call-done = bf16[32768,128]{0,1:T(8,128)(2,1)} async-done(((bf16[1024,128]{0,1:T(8,128)(2,1)}), bf16[32768,128]{0,1:T(8,128)(2,1)}) %all-gather.2.cloned.1.call-update) | async-done | bytes 8388624 | tf_op jit(solution)/shard_map/all_gather | solution.py:103
  125.9 80.3 %while.14 = (s32[]{:T(128)}, f32[1024,128]{1,0:T(8,128)S(1)}, bf16[32768,128]{0,1:T(8,128)(2,1)}, bf16[1024,64]{1,0:T(8,128)(2,1)S(1)}, s32[]{:T(128)}, /*index=5*/s32[]{:T(128)}, s32[]{:T(128)}, s32[]{:T(128)}, s32[]{}) while((s32[]{:T(128)}, f32[1024,128]{1,0:T(8,128)S(1)}, bf16[32768,128]{0,1:T(8,128)(2,1)}, ...), condition=%wide.region_4.5_spmd.clone, body=%wide.region_3.4_spmd.clone.sunk | while | flops 807665664 | bytes 2752681 | solution.py:117
  125.9 1.0 dynamic-slice.8
  126.9 0.3 copy.93
  127.2 3.7 %fusion.47 = f32[1024,128]{1,0:T(8,128)S(1)} fusion(bf16[1024,64]{1,0:T(8,128)(2,1)S(1)} %get-tuple-element.180, f32[1024,128]{1,0:T(8,128)S(1)} %get-tuple-element.169, bf16[2048,64]{1,0:T(8,128)(2,1)S(1)} %copy.93, bf16[32768,128]{0,1:T(8,128)(2,1)} %get-tuple-element.179, s32[]{:T(128)S(6)} %select_n.73, pred[]{:T(512)S(6)} %compare.11), kind=kOutput, calls=%fused_computation.6.clone.1 | convolution fusion | flops 807665664 | bytes 1703941 | tf_op jit(solution)/shard_map/while/body/eval_jaxpr/dot_general | solution.py:115
  130.9 1.0 dynamic-slice.8
  132.2 3.7 %fusion.47 = f32[1024,128]{1,0:T(8,128)S(1)} fusion(bf16[1024,64]{1,0:T(8,128)(2,1)S(1)} %get-tuple-element.180, f32[1024,128]{1,0:T(8,128)S(1)} %get-tuple-element.169, bf16[2048,64]{1,0:T(8,128)(2,1)S(1)} %copy.93, bf16[32768,128]{0,1:T(8,128)(2,1)} %get-tuple-element.179, s32[]{:T(128)S(6)} %select_n.73, pred[]{:T(512)S(6)} %compare.11), kind=kOutput, calls=%fused_computation.6.clone.1 | convolution fusion | flops 807665664 | bytes 1703941 | tf_op jit(solution)/shard_map/while/body/eval_jaxpr/dot_general | solution.py:115
  135.9 1.0 dynamic-slice.8
  137.2 3.7 %fusion.47 = f32[1024,128]{1,0:T(8,128)S(1)} fusion(bf16[1024,64]{1,0:T(8,128)(2,1)S(1)} %get-tuple-element.180, f32[1024,128]{1,0:T(8,128)S(1)} %get-tuple-element.169, bf16[2048,64]{1,0:T(8,128)(2,1)S(1)} %copy.93, bf16[32768,128]{0,1:T(8,128)(2,1)} %get-tuple-element.179, s32[]{:T(128)S(6)} %select_n.73, pred[]{:T(512)S(6)} %compare.11), kind=kOutput, calls=%fused_computation.6.clone.1 | convolution fusion | flops 807665664 | bytes 1703941 | tf_op jit(solution)/shard_map/while/body/eval_jaxpr/dot_general | solution.py:115
  140.9 1.0 dynamic-slice.8
  142.2 3.7 %fusion.47 = f32[1024,128]{1,0:T(8,128)S(1)} fusion(bf16[1024,64]{1,0:T(8,128)(2,1)S(1)} %get-tuple-element.180, f32[1024,128]{1,0:T(8,128)S(1)} %get-tuple-element.169, bf16[2048,64]{1,0:T(8,128)(2,1)S(1)} %copy.93, bf16[32768,128]{0,1:T(8,128)(2,1)} %get-tuple-element.179, s32[]{:T(128)S(6)} %select_n.73, pred[]{:T(512)S(6)} %compare.11), kind=kOutput, calls=%fused_computation.6.clone.1 | convolution fusion | flops 807665664 | bytes 1703941 | tf_op jit(solution)/shard_map/while/body/eval_jaxpr/dot_general | solution.py:115
  146.0 1.0 dynamic-slice.8
  147.2 3.7 %fusion.47 = f32[1024,128]{1,0:T(8,128)S(1)} fusion(bf16[1024,64]{1,0:T(8,128)(2,1)S(1)} %get-tuple-element.180, f32[1024,128]{1,0:T(8,128)S(1)} %get-tuple-element.169, bf16[2048,64]{1,0:T(8,128)(2,1)S(1)} %copy.93, bf16[32768,128]{0,1:T(8,128)(2,1)} %get-tuple-element.179, s32[]{:T(128)S(6)} %select_n.73, pred[]{:T(512)S(6)} %compare.11), kind=kOutput, calls=%fused_computation.6.clone.1 | convolution fusion | flops 807665664 | bytes 1703941 | tf_op jit(solution)/shard_map/while/body/eval_jaxpr/dot_general | solution.py:115
  151.0 1.0 dynamic-slice.8
  152.2 3.7 %fusion.47 = f32[1024,128]{1,0:T(8,128)S(1)} fusion(bf16[1024,64]{1,0:T(8,128)(2,1)S(1)} %get-tuple-element.180, f32[1024,128]{1,0:T(8,128)S(1)} %get-tuple-element.169, bf16[2048,64]{1,0:T(8,128)(2,1)S(1)} %copy.93, bf16[32768,128]{0,1:T(8,128)(2,1)} %get-tuple-element.179, s32[]{:T(128)S(6)} %select_n.73, pred[]{:T(512)S(6)} %compare.11), kind=kOutput, calls=%fused_computation.6.clone.1 | convolution fusion | flops 807665664 | bytes 1703941 | tf_op jit(solution)/shard_map/while/body/eval_jaxpr/dot_general | solution.py:115
  156.0 1.0 dynamic-slice.8
  157.3 3.7 %fusion.47 = f32[1024,128]{1,0:T(8,128)S(1)} fusion(bf16[1024,64]{1,0:T(8,128)(2,1)S(1)} %get-tuple-element.180, f32[1024,128]{1,0:T(8,128)S(1)} %get-tuple-element.169, bf16[2048,64]{1,0:T(8,128)(2,1)S(1)} %copy.93, bf16[32768,128]{0,1:T(8,128)(2,1)} %get-tuple-element.179, s32[]{:T(128)S(6)} %select_n.73, pred[]{:T(512)S(6)} %compare.11), kind=kOutput, calls=%fused_computation.6.clone.1 | convolution fusion | flops 807665664 | bytes 1703941 | tf_op jit(solution)/shard_map/while/body/eval_jaxpr/dot_general | solution.py:115
  161.0 1.0 dynamic-slice.8
  162.3 3.7 %fusion.47 = f32[1024,128]{1,0:T(8,128)S(1)} fusion(bf16[1024,64]{1,0:T(8,128)(2,1)S(1)} %get-tuple-element.180, f32[1024,128]{1,0:T(8,128)S(1)} %get-tuple-element.169, bf16[2048,64]{1,0:T(8,128)(2,1)S(1)} %copy.93, bf16[32768,128]{0,1:T(8,128)(2,1)} %get-tuple-element.179, s32[]{:T(128)S(6)} %select_n.73, pred[]{:T(512)S(6)} %compare.11), kind=kOutput, calls=%fused_computation.6.clone.1 | convolution fusion | flops 807665664 | bytes 1703941 | tf_op jit(solution)/shard_map/while/body/eval_jaxpr/dot_general | solution.py:115
  166.0 1.0 dynamic-slice.8
  167.3 3.7 %fusion.47 = f32[1024,128]{1,0:T(8,128)S(1)} fusion(bf16[1024,64]{1,0:T(8,128)(2,1)S(1)} %get-tuple-element.180, f32[1024,128]{1,0:T(8,128)S(1)} %get-tuple-element.169, bf16[2048,64]{1,0:T(8,128)(2,1)S(1)} %copy.93, bf16[32768,128]{0,1:T(8,128)(2,1)} %get-tuple-element.179, s32[]{:T(128)S(6)} %select_n.73, pred[]{:T(512)S(6)} %compare.11), kind=kOutput, calls=%fused_computation.6.clone.1 | convolution fusion | flops 807665664 | bytes 1703941 | tf_op jit(solution)/shard_map/while/body/eval_jaxpr/dot_general | solution.py:115
  171.1 1.0 dynamic-slice.8
  172.3 3.7 %fusion.47 = f32[1024,128]{1,0:T(8,128)S(1)} fusion(bf16[1024,64]{1,0:T(8,128)(2,1)S(1)} %get-tuple-element.180, f32[1024,128]{1,0:T(8,128)S(1)} %get-tuple-element.169, bf16[2048,64]{1,0:T(8,128)(2,1)S(1)} %copy.93, bf16[32768,128]{0,1:T(8,128)(2,1)} %get-tuple-element.179, s32[]{:T(128)S(6)} %select_n.73, pred[]{:T(512)S(6)} %compare.11), kind=kOutput, calls=%fused_computation.6.clone.1 | convolution fusion | flops 807665664 | bytes 1703941 | tf_op jit(solution)/shard_map/while/body/eval_jaxpr/dot_general | solution.py:115
  176.1 1.0 dynamic-slice.8
  177.3 3.7 %fusion.47 = f32[1024,128]{1,0:T(8,128)S(1)} fusion(bf16[1024,64]{1,0:T(8,128)(2,1)S(1)} %get-tuple-element.180, f32[1024,128]{1,0:T(8,128)S(1)} %get-tuple-element.169, bf16[2048,64]{1,0:T(8,128)(2,1)S(1)} %copy.93, bf16[32768,128]{0,1:T(8,128)(2,1)} %get-tuple-element.179, s32[]{:T(128)S(6)} %select_n.73, pred[]{:T(512)S(6)} %compare.11), kind=kOutput, calls=%fused_computation.6.clone.1 | convolution fusion | flops 807665664 | bytes 1703941 | tf_op jit(solution)/shard_map/while/body/eval_jaxpr/dot_general | solution.py:115
  181.1 1.0 dynamic-slice.8
  182.4 3.7 %fusion.47 = f32[1024,128]{1,0:T(8,128)S(1)} fusion(bf16[1024,64]{1,0:T(8,128)(2,1)S(1)} %get-tuple-element.180, f32[1024,128]{1,0:T(8,128)S(1)} %get-tuple-element.169, bf16[2048,64]{1,0:T(8,128)(2,1)S(1)} %copy.93, bf16[32768,128]{0,1:T(8,128)(2,1)} %get-tuple-element.179, s32[]{:T(128)S(6)} %select_n.73, pred[]{:T(512)S(6)} %compare.11), kind=kOutput, calls=%fused_computation.6.clone.1 | convolution fusion | flops 807665664 | bytes 1703941 | tf_op jit(solution)/shard_map/while/body/eval_jaxpr/dot_general | solution.py:115
  186.1 1.0 dynamic-slice.8
  187.4 3.7 %fusion.47 = f32[1024,128]{1,0:T(8,128)S(1)} fusion(bf16[1024,64]{1,0:T(8,128)(2,1)S(1)} %get-tuple-element.180, f32[1024,128]{1,0:T(8,128)S(1)} %get-tuple-element.169, bf16[2048,64]{1,0:T(8,128)(2,1)S(1)} %copy.93, bf16[32768,128]{0,1:T(8,128)(2,1)} %get-tuple-element.179, s32[]{:T(128)S(6)} %select_n.73, pred[]{:T(512)S(6)} %compare.11), kind=kOutput, calls=%fused_computation.6.clone.1 | convolution fusion | flops 807665664 | bytes 1703941 | tf_op jit(solution)/shard_map/while/body/eval_jaxpr/dot_general | solution.py:115
  191.1 1.0 dynamic-slice.8
  192.4 3.7 %fusion.47 = f32[1024,128]{1,0:T(8,128)S(1)} fusion(bf16[1024,64]{1,0:T(8,128)(2,1)S(1)} %get-tuple-element.180, f32[1024,128]{1,0:T(8,128)S(1)} %get-tuple-element.169, bf16[2048,64]{1,0:T(8,128)(2,1)S(1)} %copy.93, bf16[32768,128]{0,1:T(8,128)(2,1)} %get-tuple-element.179, s32[]{:T(128)S(6)} %select_n.73, pred[]{:T(512)S(6)} %compare.11), kind=kOutput, calls=%fused_computation.6.clone.1 | convolution fusion | flops 807665664 | bytes 1703941 | tf_op jit(solution)/shard_map/while/body/eval_jaxpr/dot_general | solution.py:115
  196.2 1.0 dynamic-slice.8
  197.4 3.7 %fusion.47 = f32[1024,128]{1,0:T(8,128)S(1)} fusion(bf16[1024,64]{1,0:T(8,128)(2,1)S(1)} %get-tuple-element.180, f32[1024,128]{1,0:T(8,128)S(1)} %get-tuple-element.169, bf16[2048,64]{1,0:T(8,128)(2,1)S(1)} %copy.93, bf16[32768,128]{0,1:T(8,128)(2,1)} %get-tuple-element.179, s32[]{:T(128)S(6)} %select_n.73, pred[]{:T(512)S(6)} %compare.11), kind=kOutput, calls=%fused_computation.6.clone.1 | convolution fusion | flops 807665664 | bytes 1703941 | tf_op jit(solution)/shard_map/while/body/eval_jaxpr/dot_general | solution.py:115
  201.2 1.0 dynamic-slice.8
  202.4 3.7 %fusion.47 = f32[1024,128]{1,0:T(8,128)S(1)} fusion(bf16[1024,64]{1,0:T(8,128)(2,1)S(1)} %get-tuple-element.180, f32[1024,128]{1,0:T(8,128)S(1)} %get-tuple-element.169, bf16[2048,64]{1,0:T(8,128)(2,1)S(1)} %copy.93, bf16[32768,128]{0,1:T(8,128)(2,1)} %get-tuple-element.179, s32[]{:T(128)S(6)} %select_n.73, pred[]{:T(512)S(6)} %compare.11), kind=kOutput, calls=%fused_computation.6.clone.1 | convolution fusion | flops 807665664 | bytes 1703941 | tf_op jit(solution)/shard_map/while/body/eval_jaxpr/dot_general | solution.py:115
  206.4 0.4 slice_reduce_fusion
  206.8 0.7 copy_bitcast_fusion.1
  207.5 5.4 %all-to-all-start.1 = ((bf16[8,128,64]{1,2,0:T(8,128)(2,1)}), bf16[8,128,64]{1,2,0:T(8,128)(2,1)S(1)}, u32[]{:S(2)}, u32[]{:S(2)}) async-start(bf16[8,128,64]{1,2,0:T(8,128)(2,1)} %copy_bitcast_fusion.1), calls=%async_computation.1 | async-start | bytes 262144 | tf_op jit(solution)/shard_map/all_to_all | solution.py:126
  212.8 5.3 %all-to-all-done.1 = bf16[8,128,64]{1,2,0:T(8,128)(2,1)S(1)} async-done(((bf16[8,128,64]{1,2,0:T(8,128)(2,1)}), bf16[8,128,64]{1,2,0:T(8,128)(2,1)S(1)}, u32[]{:S(2)}, u32[]{:S(2)}) %all-to-all-start.1) | async-done | bytes 131104 | tf_op jit(solution)/shard_map/all_to_all | solution.py:126
  218.1 0.6 gather_fusion.2
  218.7 0.3 multiply_reduce_fusion
  219.1 0.8 add_convert_fusion
  (88 shorter events, 7.6 us)
Async XLA Ops:
  6.5 59.8 %copy-start = (bf16[512,1024]{1,0:T(8,128)(2,1)S(1)}, bf16[512,1024]{1,0:T(8,128)(2,1)}, u32[]{:S(2)}) copy-start(bf16[512,1024]{1,0:T(8,128)(2,1)} %param.22) | copy-start | bytes 3145732
  6.5 2.8 %copy-start.11 = (f32[8]{0:T(128)S(1)}, f32[8]{0:T(128)}, u32[]{:S(2)}) copy-start(f32[8]{0:T(128)} %param.24) | copy-start | bytes 100
  6.5 119.4 %all-gather.2.cloned.1.call-start = ((), (), s32[]{:S(2)}) async-start(), calls=%async_computation.2 | async-start | bytes 8650752 | tf_op jit(solution)/shard_map/all_gather | solution.py:103
  7.6 2.1 copy-start.1
  7.6 2.1 copy-start.6
  9.7 1.0 copy-start.5
  10.1 1.0 copy-start.10
  11.8 28.8 %copy-start.12 = (s32[1,1,12]{2,1,0:T(1,128)S(1)}, s32[1,1,12]{2,1,0:T(1,128)}, u32[]{:S(2)}) copy-start(s32[1,1,12]{2,1,0:T(1,128)} %param.16) | copy-start | bytes 148
  25.7 18.2 %copy-start.2 = (bf16[1024,192]{0,1:T(8,128)(2,1)}, bf16[1024,192]{0,1:T(8,128)(2,1)S(1)}, u32[]{:S(2)}) copy-start(bf16[1024,192]{0,1:T(8,128)(2,1)S(1)} %copy_bitcast_fusion) | copy-start | bytes 1179652
  26.5 4.4 %collective-permute-start = (bf16[128,512]{1,0:T(8,128)(2,1)S(1)}, bf16[128,512]{1,0:T(8,128)(2,1)S(1)}, u32[]{:S(2)}, u32[]{:S(2)}) collective-permute-start(bf16[128,512]{1,0:T(8,128)(2,1)S(1)} %copy-done.1), channel_id=1, source_target_pairs={{0,4},{4,8},{8,12},{12,16},{16,20},{20,24},{24,28},{28,32},{32,36}... | collective-permute-start | bytes 393224 | tf_op jit(solution)/shard_map/ppermute | solution.py:26
  29.0 8.3 %collective-permute-start.1 = (bf16[128,512]{1,0:T(8,128)(2,1)S(1)}, bf16[128,512]{1,0:T(8,128)(2,1)S(1)}, u32[]{:S(2)}, u32[]{:S(2)}) collective-permute-start(bf16[128,512]{1,0:T(8,128)(2,1)S(1)} %copy-done.1), channel_id=1, source_target_pairs={{4,0},{8,4},{12,8},{16,12},{20,16},{24,20},{28,24},{32,28},{36,32}... | collective-permute-start | bytes 393224 | tf_op jit(solution)/shard_map/ppermute | solution.py:27
  37.4 21.4 %copy-start.4 = (bf16[384,512]{1,0:T(8,128)(2,1)}, bf16[384,512]{1,0:T(8,128)(2,1)S(1)}, u32[]{:S(2)}) copy-start(bf16[384,512]{1,0:T(8,128)(2,1)S(1)} %constant_dynamic-update-slice_fusion) | copy-start | bytes 1179652
  37.4 10.3 %collective-permute-start.2 = (bf16[384,512]{1,0:T(8,128)(2,1)S(1)}, bf16[384,512]{1,0:T(8,128)(2,1)}, u32[]{:S(2)}, u32[]{:S(2)}) collective-permute-start(bf16[384,512]{1,0:T(8,128)(2,1)S(1)} %constant_dynamic-update-slice_fusion), channel_id=1, source_target_pairs={{0,1},{1,2},{2,3},{3,0},{4,5},{5,6},{6,7},{7,4},{8,9},{9,10},{10,1... | collective-permute-start | bytes 1179656 | tf_op jit(solution)/shard_map/ppermute | solution.py:64
  39.4 18.7 %collective-permute-start.3 = (bf16[384,512]{1,0:T(8,128)(2,1)S(1)}, bf16[384,512]{1,0:T(8,128)(2,1)}, u32[]{:S(2)}, u32[]{:S(2)}) collective-permute-start(bf16[384,512]{1,0:T(8,128)(2,1)S(1)} %constant_dynamic-update-slice_fusion), channel_id=1, source_target_pairs={{0,2},{1,3},{2,0},{3,1},{4,6},{5,7},{6,4},{7,5},{8,10},{9,11},{10,... | collective-permute-start | bytes 1179656 | tf_op jit(solution)/shard_map/ppermute | solution.py:64
  40.6 18.2 %collective-permute-start.4 = (bf16[384,512]{1,0:T(8,128)(2,1)S(1)}, bf16[384,512]{1,0:T(8,128)(2,1)}, u32[]{:S(2)}, u32[]{:S(2)}) collective-permute-start(bf16[384,512]{1,0:T(8,128)(2,1)S(1)} %constant_dynamic-update-slice_fusion), channel_id=1, source_target_pairs={{0,3},{1,0},{2,1},{3,2},{4,7},{5,4},{6,5},{7,6},{8,11},{9,8},{10,9... | collective-permute-start | bytes 1179656 | tf_op jit(solution)/shard_map/ppermute | solution.py:64
  66.3 2.4 %copy-start.3 = (bf16[1024,512]{1,0:T(8,128)(2,1)S(1)}, bf16[1024,512]{1,0:T(8,128)(2,1)}, u32[]{:S(2)}) copy-start(bf16[1024,512]{1,0:T(8,128)(2,1)} %param.23) | copy-start | bytes 3145732
  68.7 0.9 slice-start
  206.2 6.7 %copy-start.9 = (s32[8]{0:T(128)S(1)}, s32[8]{0:T(128)}, u32[]{:S(2)}) copy-start(s32[8]{0:T(128)} %constant.122) | copy-start | bytes 100
  206.2 12.5 %copy-start.7 = (bf16[512,512]{1,0:T(8,128)(2,1)S(1)}, bf16[512,512]{1,0:T(8,128)(2,1)}, u32[]{:S(2)}) copy-start(bf16[512,512]{1,0:T(8,128)(2,1)} %param.21) | copy-start | bytes 1572868
  206.4 12.6 %copy-start.8 = (f32[512]{0:T(512)S(1)}, f32[512]{0:T(512)}, u32[]{:S(2)}) copy-start(f32[512]{0:T(512)} %param.25) | copy-start | bytes 6148
  207.5 10.6 %all-to-all-start.1 = ((bf16[8,128,64]{1,2,0:T(8,128)(2,1)}), bf16[8,128,64]{1,2,0:T(8,128)(2,1)S(1)}, u32[]{:S(2)}, u32[]{:S(2)}) async-start(bf16[8,128,64]{1,2,0:T(8,128)(2,1)} %copy_bitcast_fusion.1), calls=%async_computation.1 | async-start | bytes 262144 | tf_op jit(solution)/shard_map/all_to_all | solution.py:126
Sparse Core Ops, SparseCore 0:
  26.6 99.2 all-gather.1
where the time goes:
time: 228 us; the launch traced here: 227 us
  waiting for transfers between devices  83.2 us (36%)
  matrix products  64.5 us (28%)
  local copies, waits for them, and re-layouts  34.1 us (15%)
  blocking collectives  13.9 us (6%)
  between operations  13.8 us (6%)
  starting transfers between devices  12.4 us (5%)
  other arithmetic  4.14 us (2%)
    dot_general x16, matrix products, accumulate(): jnp.dot(weights, widened, preferred_element_type=jnp.float32)  59.7 us
    all_gather x1, waiting for transfers between devices, shards(): kv_in = lax.all_gather(key_values, (ROW, COLUMN), axis=0, tiled=True)  56.1 us
    slice x16, local copies, waits for them, and re-layouts, accumulate(): widened = jnp.concatenate([block[:, SUBSPACE_WIDTH:], ones], axis=1)  15.6 us
    ppermute x3, waiting for transfers between devices, shards(): gathered.append(lax.ppermute(halo_rows, 'head', pairs))  14.8 us
    all_to_all x1, blocking collectives, shards(): lax.all_to_all(packed, GROUP, split_axis=1, concat_axis=0, tiled=True)  13.9 us
    ppermute x1, waiting for transfers between devices, extended(): after = lax.ppermute(first, DOM, down)  6.36 us
    all_to_all x1, starting transfers between devices, shards(): lax.all_to_all(merged, GROUP, split_axis=0, concat_axis=1, tiled=True)  5.36 us
    all_to_all x1, waiting for transfers between devices, shards(): lax.all_to_all(merged, GROUP, split_axis=0, concat_axis=1, tiled=True)  5.26 us
  transfers between devices with their start and end apart: 7, of which 7 were waited for; matrix products, arithmetic and copies ran while one was open for 6% of the time, Pallas kernels for 0%

commit v1 on v0

--- a/solution.py
+++ b/solution.py
@@ -123,7 +123,10 @@
     merged = (totals[:, :SUBSPACE_WIDTH] / totals[:, SUBSPACE_WIDTH : SUBSPACE_WIDTH + 1]).astype(
         jnp.bfloat16
     )
-    back = lax.all_to_all(merged, GROUP, split_axis=0, concat_axis=1, tiled=True)
+    back = jnp.concatenate(
+        lax.all_to_all(jnp.stack(jnp.split(merged, lax.axis_size(GROUP), axis=0)), GROUP, 0, 0),
+        axis=1,
+    )
     node_heads = back.reshape(block_len, members, SUBSPACE_WIDTH)[:, jnp.array(member_of)]
     node_heads = node_heads.reshape(block_len, -1)
     attended = jnp.dot(node_heads, final_projector, preferred_element_type=jnp.float32)

time: 228 us -> 232 us (1.018)
  local copies, waits for them, and re-layouts: 34.1 us -> 39 us
    unnamed x29 -> x36, local copies, waits for them, and re-layouts: 0.52 us -> 4.8 us
where the time goes in v1:
time: 232 us; the launch traced here: 231 us
  waiting for transfers between devices  83.2 us (36%)
  matrix products  64.5 us (28%)
  local copies, waits for them, and re-layouts  39 us (17%)
  blocking collectives  13.9 us (6%)
  between operations  13.8 us (6%)
  starting transfers between devices  12.4 us (5%)
  other arithmetic  3.48 us (2%)
    dot_general x16, matrix products, accumulate(): jnp.dot(weights, widened, preferred_element_type=jnp.float32)  59.7 us
    all_gather x1, waiting for transfers between devices, shards(): kv_in = lax.all_gather(key_values, (ROW, COLUMN), axis=0, tiled=True)  56.1 us
    slice x16, local copies, waits for them, and re-layouts, accumulate(): widened = jnp.concatenate([block[:, SUBSPACE_WIDTH:], ones], axis=1)  15.6 us
    ppermute x3, waiting for transfers between devices, shards(): gathered.append(lax.ppermute(halo_rows, 'head', pairs))  14.8 us
    all_to_all x1, blocking collectives, shards(): lax.all_to_all(packed, GROUP, split_axis=1, concat_axis=0, tiled=True)  13.9 us
    ppermute x1, waiting for transfers between devices, extended(): after = lax.ppermute(first, DOM, down)  6.36 us
    all_to_all x1, starting transfers between devices, shards(): lax.all_to_all(jnp.stack(jnp.split(merged, lax.axis_size(GROUP), axis=0))...  5.36 us
    all_to_all x1, waiting for transfers between devices, shards(): lax.all_to_all(jnp.stack(jnp.split(merged, lax.axis_size(GROUP), axis=0))...  5.26 us
  transfers between devices with their start and end apart: 7, of which 7 were waited for; matrix products, arithmetic and copies ran while one was open for 6% of the time, Pallas kernels for 0%

profile of v1, /device:TPU:1, one launch (start us, length us, event | category | flops | bytes accessed | tf_op | source)
XLA Modules:
  0.0 230.9 jit_solution(11637859349614036254)
XLA Ops:
  6.5 0.8 maximum_reduce_fusion
  7.6 1.4 fusion.21
  11.2 0.6 gather_fusion.1
  11.8 13.9 %all_to_all.24 = bf16[128,8,192]{0,2,1:T(8,128)(2,1)S(1)} all-to-all(bf16[128,8,192]{0,2,1:T(8,128)(2,1)S(1)} %bitcast.90), channel_id=1, replica_groups=mesh['x'=4,'z'=8,'yhi'=2,'head'=4] {'yhi','head'}, dimensions={1} | all-to-all | bytes 786432 | tf_op jit(solution)/shard_map/all_to_all | solution.py:90
  25.7 0.8 slice.39
  26.5 2.5 %collective-permute-start = (bf16[128,512]{1,0:T(8,128)(2,1)S(1)}, bf16[128,512]{1,0:T(8,128)(2,1)S(1)}, u32[]{:S(2)}, u32[]{:S(2)}) collective-permute-start(bf16[128,512]{1,0:T(8,128)(2,1)S(1)} %copy-done.1), channel_id=1, source_target_pairs={{0,4},{4,8},{8,12},{12,16},{16,20},{20,24},{24,28},{28,32},{32,36}... | collective-permute-start | bytes 393224 | tf_op jit(solution)/shard_map/ppermute | solution.py:26
  29.0 1.3 collective-permute-start.1
  30.3 0.6 collective-permute-done
  31.0 6.4 %collective-permute-done.1 = bf16[128,512]{1,0:T(8,128)(2,1)S(1)} collective-permute-done((bf16[128,512]{1,0:T(8,128)(2,1)S(1)}, bf16[128,512]{1,0:T(8,128)(2,1)S(1)}, u32[]{:S(2)}, u32[]{:S(2)}) %collective-permute-start.1) | collective-permute-done | bytes 131104 | tf_op jit(solution)/shard_map/ppermute | solution.py:27
  37.4 2.0 collective-permute-start.2
  39.4 1.2 collective-permute-start.3
  41.2 1.7 gather_fusion
  43.0 1.0 copy.33
  44.0 3.7 %collective-permute-done.2 = bf16[384,512]{1,0:T(8,128)(2,1)} collective-permute-done((bf16[384,512]{1,0:T(8,128)(2,1)S(1)}, bf16[384,512]{1,0:T(8,128)(2,1)}, u32[]{:S(2)}, u32[]{:S(2)}) %collective-permute-start.2) | collective-permute-done | bytes 393248 | tf_op jit(solution)/shard_map/ppermute | solution.py:64
  47.7 10.4 %collective-permute-done.3 = bf16[384,512]{1,0:T(8,128)(2,1)} collective-permute-done((bf16[384,512]{1,0:T(8,128)(2,1)S(1)}, bf16[384,512]{1,0:T(8,128)(2,1)}, u32[]{:S(2)}, u32[]{:S(2)}) %collective-permute-start.3) | collective-permute-done | bytes 393248 | tf_op jit(solution)/shard_map/ppermute | solution.py:64
  58.1 0.6 collective-permute-done.4
  58.8 1.6 pad_maximum_fusion
  60.3 1.3 broadcast_in_dim.47
  61.7 4.7 %scatter_fusion = bf16[4,384,512]{2,1,0:T(8,128)(2,1)} fusion(bf16[4,384,512]{2,1,0:T(8,128)(2,1)} %broadcast_in_dim.47, s32[4]{0:T(128)S(1)} %fusion.19, bf16[4,384,512]{2,1,0:T(8,128)(2,1)S(1)} %pad_maximum_fusion), kind=kCustom, calls=%fused_computation.3 | custom fusion | bytes 4718608 | tf_op jit(solution)/shard_map/scatter | solution.py:67
  66.4 2.3 %fusion.16 = bf16[128,1024]{1,0:T(8,128)(2,1)S(1)} fusion(bf16[512,1024]{1,0:T(8,128)(2,1)S(1)} %copy-done, bf16[128,1536]{0,1:T(8,128)(2,1)} %bitcast.99, bf16[1536,512]{1,0:T(8,128)(2,1)} %bitcast.89), kind=kOutput, calls=%fused_computation.23 | convolution fusion | flops 336789504 | bytes 3276800 | tf_op jit(solution)/shard_map/dot_general | solution.py:99
  69.8 56.1 %all-gather.2.cloned.1.call-done = bf16[32768,128]{0,1:T(8,128)(2,1)} async-done(((bf16[1024,128]{0,1:T(8,128)(2,1)}), bf16[32768,128]{0,1:T(8,128)(2,1)}) %all-gather.2.cloned.1.call-update) | async-done | bytes 8388624 | tf_op jit(solution)/shard_map/all_gather | solution.py:103
  125.9 80.3 %while.14 = (s32[]{:T(128)}, f32[1024,128]{1,0:T(8,128)S(1)}, bf16[32768,128]{0,1:T(8,128)(2,1)}, bf16[1024,64]{1,0:T(8,128)(2,1)S(1)}, s32[]{:T(128)}, /*index=5*/s32[]{:T(128)}, s32[]{:T(128)}, s32[]{:T(128)}, s32[]{}) while((s32[]{:T(128)}, f32[1024,128]{1,0:T(8,128)S(1)}, bf16[32768,128]{0,1:T(8,128)(2,1)}, ...), condition=%wide.region_4.5_spmd.clone, body=%wide.region_3.4_spmd.clone.sunk | while | flops 807665664 | bytes 2752681 | solution.py:117
  125.9 1.0 dynamic-slice.8
  127.2 3.7 %fusion.45 = f32[1024,128]{1,0:T(8,128)S(1)} fusion(bf16[1024,64]{1,0:T(8,128)(2,1)S(1)} %get-tuple-element.172, f32[1024,128]{1,0:T(8,128)S(1)} %get-tuple-element.161, bf16[2048,64]{1,0:T(8,128)(2,1)S(1)} %copy.54, bf16[32768,128]{0,1:T(8,128)(2,1)} %get-tuple-element.171, s32[]{:T(128)S(6)} %select_n.73, pred[]{:T(512)S(6)} %compare.11), kind=kOutput, calls=%fused_computation.6.clone.1 | convolution fusion | flops 807665664 | bytes 1703941 | tf_op jit(solution)/shard_map/while/body/eval_jaxpr/dot_general | solution.py:115
  130.9 1.0 dynamic-slice.8
  132.2 3.7 %fusion.45 = f32[1024,128]{1,0:T(8,128)S(1)} fusion(bf16[1024,64]{1,0:T(8,128)(2,1)S(1)} %get-tuple-element.172, f32[1024,128]{1,0:T(8,128)S(1)} %get-tuple-element.161, bf16[2048,64]{1,0:T(8,128)(2,1)S(1)} %copy.54, bf16[32768,128]{0,1:T(8,128)(2,1)} %get-tuple-element.171, s32[]{:T(128)S(6)} %select_n.73, pred[]{:T(512)S(6)} %compare.11), kind=kOutput, calls=%fused_computation.6.clone.1 | convolution fusion | flops 807665664 | bytes 1703941 | tf_op jit(solution)/shard_map/while/body/eval_jaxpr/dot_general | solution.py:115
  135.9 1.0 dynamic-slice.8
  137.2 3.7 %fusion.45 = f32[1024,128]{1,0:T(8,128)S(1)} fusion(bf16[1024,64]{1,0:T(8,128)(2,1)S(1)} %get-tuple-element.172, f32[1024,128]{1,0:T(8,128)S(1)} %get-tuple-element.161, bf16[2048,64]{1,0:T(8,128)(2,1)S(1)} %copy.54, bf16[32768,128]{0,1:T(8,128)(2,1)} %get-tuple-element.171, s32[]{:T(128)S(6)} %select_n.73, pred[]{:T(512)S(6)} %compare.11), kind=kOutput, calls=%fused_computation.6.clone.1 | convolution fusion | flops 807665664 | bytes 1703941 | tf_op jit(solution)/shard_map/while/body/eval_jaxpr/dot_general | solution.py:115
  140.9 1.0 dynamic-slice.8
  142.2 3.7 %fusion.45 = f32[1024,128]{1,0:T(8,128)S(1)} fusion(bf16[1024,64]{1,0:T(8,128)(2,1)S(1)} %get-tuple-element.172, f32[1024,128]{1,0:T(8,128)S(1)} %get-tuple-element.161, bf16[2048,64]{1,0:T(8,128)(2,1)S(1)} %copy.54, bf16[32768,128]{0,1:T(8,128)(2,1)} %get-tuple-element.171, s32[]{:T(128)S(6)} %select_n.73, pred[]{:T(512)S(6)} %compare.11), kind=kOutput, calls=%fused_computation.6.clone.1 | convolution fusion | flops 807665664 | bytes 1703941 | tf_op jit(solution)/shard_map/while/body/eval_jaxpr/dot_general | solution.py:115
  146.0 1.0 dynamic-slice.8
  147.2 3.7 %fusion.45 = f32[1024,128]{1,0:T(8,128)S(1)} fusion(bf16[1024,64]{1,0:T(8,128)(2,1)S(1)} %get-tuple-element.172, f32[1024,128]{1,0:T(8,128)S(1)} %get-tuple-element.161, bf16[2048,64]{1,0:T(8,128)(2,1)S(1)} %copy.54, bf16[32768,128]{0,1:T(8,128)(2,1)} %get-tuple-element.171, s32[]{:T(128)S(6)} %select_n.73, pred[]{:T(512)S(6)} %compare.11), kind=kOutput, calls=%fused_computation.6.clone.1 | convolution fusion | flops 807665664 | bytes 1703941 | tf_op jit(solution)/shard_map/while/body/eval_jaxpr/dot_general | solution.py:115
  151.0 1.0 dynamic-slice.8
  152.2 3.7 %fusion.45 = f32[1024,128]{1,0:T(8,128)S(1)} fusion(bf16[1024,64]{1,0:T(8,128)(2,1)S(1)} %get-tuple-element.172, f32[1024,128]{1,0:T(8,128)S(1)} %get-tuple-element.161, bf16[2048,64]{1,0:T(8,128)(2,1)S(1)} %copy.54, bf16[32768,128]{0,1:T(8,128)(2,1)} %get-tuple-element.171, s32[]{:T(128)S(6)} %select_n.73, pred[]{:T(512)S(6)} %compare.11), kind=kOutput, calls=%fused_computation.6.clone.1 | convolution fusion | flops 807665664 | bytes 1703941 | tf_op jit(solution)/shard_map/while/body/eval_jaxpr/dot_general | solution.py:115
  156.0 1.0 dynamic-slice.8
  157.3 3.7 %fusion.45 = f32[1024,128]{1,0:T(8,128)S(1)} fusion(bf16[1024,64]{1,0:T(8,128)(2,1)S(1)} %get-tuple-element.172, f32[1024,128]{1,0:T(8,128)S(1)} %get-tuple-element.161, bf16[2048,64]{1,0:T(8,128)(2,1)S(1)} %copy.54, bf16[32768,128]{0,1:T(8,128)(2,1)} %get-tuple-element.171, s32[]{:T(128)S(6)} %select_n.73, pred[]{:T(512)S(6)} %compare.11), kind=kOutput, calls=%fused_computation.6.clone.1 | convolution fusion | flops 807665664 | bytes 1703941 | tf_op jit(solution)/shard_map/while/body/eval_jaxpr/dot_general | solution.py:115
  161.0 1.0 dynamic-slice.8
  162.3 3.7 %fusion.45 = f32[1024,128]{1,0:T(8,128)S(1)} fusion(bf16[1024,64]{1,0:T(8,128)(2,1)S(1)} %get-tuple-element.172, f32[1024,128]{1,0:T(8,128)S(1)} %get-tuple-element.161, bf16[2048,64]{1,0:T(8,128)(2,1)S(1)} %copy.54, bf16[32768,128]{0,1:T(8,128)(2,1)} %get-tuple-element.171, s32[]{:T(128)S(6)} %select_n.73, pred[]{:T(512)S(6)} %compare.11), kind=kOutput, calls=%fused_computation.6.clone.1 | convolution fusion | flops 807665664 | bytes 1703941 | tf_op jit(solution)/shard_map/while/body/eval_jaxpr/dot_general | solution.py:115
  166.0 1.0 dynamic-slice.8
  167.3 3.7 %fusion.45 = f32[1024,128]{1,0:T(8,128)S(1)} fusion(bf16[1024,64]{1,0:T(8,128)(2,1)S(1)} %get-tuple-element.172, f32[1024,128]{1,0:T(8,128)S(1)} %get-tuple-element.161, bf16[2048,64]{1,0:T(8,128)(2,1)S(1)} %copy.54, bf16[32768,128]{0,1:T(8,128)(2,1)} %get-tuple-element.171, s32[]{:T(128)S(6)} %select_n.73, pred[]{:T(512)S(6)} %compare.11), kind=kOutput, calls=%fused_computation.6.clone.1 | convolution fusion | flops 807665664 | bytes 1703941 | tf_op jit(solution)/shard_map/while/body/eval_jaxpr/dot_general | solution.py:115
  171.1 1.0 dynamic-slice.8
  172.3 3.7 %fusion.45 = f32[1024,128]{1,0:T(8,128)S(1)} fusion(bf16[1024,64]{1,0:T(8,128)(2,1)S(1)} %get-tuple-element.172, f32[1024,128]{1,0:T(8,128)S(1)} %get-tuple-element.161, bf16[2048,64]{1,0:T(8,128)(2,1)S(1)} %copy.54, bf16[32768,128]{0,1:T(8,128)(2,1)} %get-tuple-element.171, s32[]{:T(128)S(6)} %select_n.73, pred[]{:T(512)S(6)} %compare.11), kind=kOutput, calls=%fused_computation.6.clone.1 | convolution fusion | flops 807665664 | bytes 1703941 | tf_op jit(solution)/shard_map/while/body/eval_jaxpr/dot_general | solution.py:115
  176.1 1.0 dynamic-slice.8
  177.3 3.7 %fusion.45 = f32[1024,128]{1,0:T(8,128)S(1)} fusion(bf16[1024,64]{1,0:T(8,128)(2,1)S(1)} %get-tuple-element.172, f32[1024,128]{1,0:T(8,128)S(1)} %get-tuple-element.161, bf16[2048,64]{1,0:T(8,128)(2,1)S(1)} %copy.54, bf16[32768,128]{0,1:T(8,128)(2,1)} %get-tuple-element.171, s32[]{:T(128)S(6)} %select_n.73, pred[]{:T(512)S(6)} %compare.11), kind=kOutput, calls=%fused_computation.6.clone.1 | convolution fusion | flops 807665664 | bytes 1703941 | tf_op jit(solution)/shard_map/while/body/eval_jaxpr/dot_general | solution.py:115
  181.1 1.0 dynamic-slice.8
  182.4 3.7 %fusion.45 = f32[1024,128]{1,0:T(8,128)S(1)} fusion(bf16[1024,64]{1,0:T(8,128)(2,1)S(1)} %get-tuple-element.172, f32[1024,128]{1,0:T(8,128)S(1)} %get-tuple-element.161, bf16[2048,64]{1,0:T(8,128)(2,1)S(1)} %copy.54, bf16[32768,128]{0,1:T(8,128)(2,1)} %get-tuple-element.171, s32[]{:T(128)S(6)} %select_n.73, pred[]{:T(512)S(6)} %compare.11), kind=kOutput, calls=%fused_computation.6.clone.1 | convolution fusion | flops 807665664 | bytes 1703941 | tf_op jit(solution)/shard_map/while/body/eval_jaxpr/dot_general | solution.py:115
  186.1 1.0 dynamic-slice.8
  187.4 3.7 %fusion.45 = f32[1024,128]{1,0:T(8,128)S(1)} fusion(bf16[1024,64]{1,0:T(8,128)(2,1)S(1)} %get-tuple-element.172, f32[1024,128]{1,0:T(8,128)S(1)} %get-tuple-element.161, bf16[2048,64]{1,0:T(8,128)(2,1)S(1)} %copy.54, bf16[32768,128]{0,1:T(8,128)(2,1)} %get-tuple-element.171, s32[]{:T(128)S(6)} %select_n.73, pred[]{:T(512)S(6)} %compare.11), kind=kOutput, calls=%fused_computation.6.clone.1 | convolution fusion | flops 807665664 | bytes 1703941 | tf_op jit(solution)/shard_map/while/body/eval_jaxpr/dot_general | solution.py:115
  191.1 1.0 dynamic-slice.8
  192.4 3.7 %fusion.45 = f32[1024,128]{1,0:T(8,128)S(1)} fusion(bf16[1024,64]{1,0:T(8,128)(2,1)S(1)} %get-tuple-element.172, f32[1024,128]{1,0:T(8,128)S(1)} %get-tuple-element.161, bf16[2048,64]{1,0:T(8,128)(2,1)S(1)} %copy.54, bf16[32768,128]{0,1:T(8,128)(2,1)} %get-tuple-element.171, s32[]{:T(128)S(6)} %select_n.73, pred[]{:T(512)S(6)} %compare.11), kind=kOutput, calls=%fused_computation.6.clone.1 | convolution fusion | flops 807665664 | bytes 1703941 | tf_op jit(solution)/shard_map/while/body/eval_jaxpr/dot_general | solution.py:115
  196.2 1.0 dynamic-slice.8
  197.4 3.7 %fusion.45 = f32[1024,128]{1,0:T(8,128)S(1)} fusion(bf16[1024,64]{1,0:T(8,128)(2,1)S(1)} %get-tuple-element.172, f32[1024,128]{1,0:T(8,128)S(1)} %get-tuple-element.161, bf16[2048,64]{1,0:T(8,128)(2,1)S(1)} %copy.54, bf16[32768,128]{0,1:T(8,128)(2,1)} %get-tuple-element.171, s32[]{:T(128)S(6)} %select_n.73, pred[]{:T(512)S(6)} %compare.11), kind=kOutput, calls=%fused_computation.6.clone.1 | convolution fusion | flops 807665664 | bytes 1703941 | tf_op jit(solution)/shard_map/while/body/eval_jaxpr/dot_general | solution.py:115
  201.2 1.0 dynamic-slice.8
  202.4 3.7 %fusion.45 = f32[1024,128]{1,0:T(8,128)S(1)} fusion(bf16[1024,64]{1,0:T(8,128)(2,1)S(1)} %get-tuple-element.172, f32[1024,128]{1,0:T(8,128)S(1)} %get-tuple-element.161, bf16[2048,64]{1,0:T(8,128)(2,1)S(1)} %copy.54, bf16[32768,128]{0,1:T(8,128)(2,1)} %get-tuple-element.171, s32[]{:T(128)S(6)} %select_n.73, pred[]{:T(512)S(6)} %compare.11), kind=kOutput, calls=%fused_computation.6.clone.1 | convolution fusion | flops 807665664 | bytes 1703941 | tf_op jit(solution)/shard_map/while/body/eval_jaxpr/dot_general | solution.py:115
  206.8 0.6 constant_dynamic-update-slice_fusion.10
  207.4 0.6 constant_dynamic-update-slice_fusion.9
  208.0 0.6 constant_dynamic-update-slice_fusion.8
  208.7 0.6 constant_dynamic-update-slice_fusion.7
  209.3 0.6 constant_dynamic-update-slice_fusion.6
  209.9 0.6 constant_dynamic-update-slice_fusion.5
  211.1 0.6 constant_dynamic-update-slice_fusion.3
  211.7 5.4 %all-to-all-start.1 = ((bf16[8,128,64]{1,2,0:T(8,128)(2,1)}), bf16[8,128,64]{1,2,0:T(8,128)(2,1)S(1)}, u32[]{:S(2)}, u32[]{:S(2)}) async-start(bf16[8,128,64]{1,2,0:T(8,128)(2,1)} %constant_dynamic-update-slice_fusion.3), calls=%async_computation.1 | async-start | bytes 262144 | tf_op jit(solution)/shard_map/all_to_all | solution.py:127
  217.1 5.3 %all-to-all-done.1 = bf16[8,128,64]{1,2,0:T(8,128)(2,1)S(1)} async-done(((bf16[8,128,64]{1,2,0:T(8,128)(2,1)}), bf16[8,128,64]{1,2,0:T(8,128)(2,1)S(1)}, u32[]{:S(2)}, u32[]{:S(2)}) %all-to-all-start.1) | async-done | bytes 131104 | tf_op jit(solution)/shard_map/all_to_all | solution.py:127
  223.3 0.8 add_convert_fusion
  (96 shorter events, 10.7 us)
Async XLA Ops:
  6.5 59.8 %copy-start = (bf16[512,1024]{1,0:T(8,128)(2,1)S(1)}, bf16[512,1024]{1,0:T(8,128)(2,1)}, u32[]{:S(2)}) copy-start(bf16[512,1024]{1,0:T(8,128)(2,1)} %param.22) | copy-start | bytes 3145732
  6.5 2.8 %copy-start.11 = (f32[8]{0:T(128)S(1)}, f32[8]{0:T(128)}, u32[]{:S(2)}) copy-start(f32[8]{0:T(128)} %param.24) | copy-start | bytes 100
  6.5 119.4 %all-gather.2.cloned.1.call-start = ((), (), s32[]{:S(2)}) async-start(), calls=%async_computation.2 | async-start | bytes 8650752 | tf_op jit(solution)/shard_map/all_gather | solution.py:103
  7.6 2.1 copy-start.1
  7.6 2.1 copy-start.6
  9.7 1.0 copy-start.5
  10.1 1.0 copy-start.10
  11.8 28.8 %copy-start.12 = (s32[1,1,12]{2,1,0:T(1,128)S(1)}, s32[1,1,12]{2,1,0:T(1,128)}, u32[]{:S(2)}) copy-start(s32[1,1,12]{2,1,0:T(1,128)} %param.16) | copy-start | bytes 148
  25.7 18.2 %copy-start.2 = (bf16[1024,192]{0,1:T(8,128)(2,1)}, bf16[1024,192]{0,1:T(8,128)(2,1)S(1)}, u32[]{:S(2)}) copy-start(bf16[1024,192]{0,1:T(8,128)(2,1)S(1)} %copy_bitcast_fusion) | copy-start | bytes 1179652
  26.5 4.4 %collective-permute-start = (bf16[128,512]{1,0:T(8,128)(2,1)S(1)}, bf16[128,512]{1,0:T(8,128)(2,1)S(1)}, u32[]{:S(2)}, u32[]{:S(2)}) collective-permute-start(bf16[128,512]{1,0:T(8,128)(2,1)S(1)} %copy-done.1), channel_id=1, source_target_pairs={{0,4},{4,8},{8,12},{12,16},{16,20},{20,24},{24,28},{28,32},{32,36}... | collective-permute-start | bytes 393224 | tf_op jit(solution)/shard_map/ppermute | solution.py:26
  29.0 8.3 %collective-permute-start.1 = (bf16[128,512]{1,0:T(8,128)(2,1)S(1)}, bf16[128,512]{1,0:T(8,128)(2,1)S(1)}, u32[]{:S(2)}, u32[]{:S(2)}) collective-permute-start(bf16[128,512]{1,0:T(8,128)(2,1)S(1)} %copy-done.1), channel_id=1, source_target_pairs={{4,0},{8,4},{12,8},{16,12},{20,16},{24,20},{28,24},{32,28},{36,32}... | collective-permute-start | bytes 393224 | tf_op jit(solution)/shard_map/ppermute | solution.py:27
  37.4 21.4 %copy-start.4 = (bf16[384,512]{1,0:T(8,128)(2,1)}, bf16[384,512]{1,0:T(8,128)(2,1)S(1)}, u32[]{:S(2)}) copy-start(bf16[384,512]{1,0:T(8,128)(2,1)S(1)} %constant_dynamic-update-slice_fusion) | copy-start | bytes 1179652
  37.4 10.3 %collective-permute-start.2 = (bf16[384,512]{1,0:T(8,128)(2,1)S(1)}, bf16[384,512]{1,0:T(8,128)(2,1)}, u32[]{:S(2)}, u32[]{:S(2)}) collective-permute-start(bf16[384,512]{1,0:T(8,128)(2,1)S(1)} %constant_dynamic-update-slice_fusion), channel_id=1, source_target_pairs={{0,1},{1,2},{2,3},{3,0},{4,5},{5,6},{6,7},{7,4},{8,9},{9,10},{10,1... | collective-permute-start | bytes 1179656 | tf_op jit(solution)/shard_map/ppermute | solution.py:64
  39.4 18.7 %collective-permute-start.3 = (bf16[384,512]{1,0:T(8,128)(2,1)S(1)}, bf16[384,512]{1,0:T(8,128)(2,1)}, u32[]{:S(2)}, u32[]{:S(2)}) collective-permute-start(bf16[384,512]{1,0:T(8,128)(2,1)S(1)} %constant_dynamic-update-slice_fusion), channel_id=1, source_target_pairs={{0,2},{1,3},{2,0},{3,1},{4,6},{5,7},{6,4},{7,5},{8,10},{9,11},{10,... | collective-permute-start | bytes 1179656 | tf_op jit(solution)/shard_map/ppermute | solution.py:64
  40.6 18.2 %collective-permute-start.4 = (bf16[384,512]{1,0:T(8,128)(2,1)S(1)}, bf16[384,512]{1,0:T(8,128)(2,1)}, u32[]{:S(2)}, u32[]{:S(2)}) collective-permute-start(bf16[384,512]{1,0:T(8,128)(2,1)S(1)} %constant_dynamic-update-slice_fusion), channel_id=1, source_target_pairs={{0,3},{1,0},{2,1},{3,2},{4,7},{5,4},{6,5},{7,6},{8,11},{9,8},{10,9... | collective-permute-start | bytes 1179656 | tf_op jit(solution)/shard_map/ppermute | solution.py:64
  66.3 2.4 %copy-start.3 = (bf16[1024,512]{1,0:T(8,128)(2,1)S(1)}, bf16[1024,512]{1,0:T(8,128)(2,1)}, u32[]{:S(2)}) copy-start(bf16[1024,512]{1,0:T(8,128)(2,1)} %param.23) | copy-start | bytes 3145732
  68.7 0.9 slice-start
  206.2 10.9 %copy-start.9 = (s32[8]{0:T(128)S(1)}, s32[8]{0:T(128)}, u32[]{:S(2)}) copy-start(s32[8]{0:T(128)} %constant.122) | copy-start | bytes 100
  206.2 16.7 %copy-start.7 = (bf16[512,512]{1,0:T(8,128)(2,1)S(1)}, bf16[512,512]{1,0:T(8,128)(2,1)}, u32[]{:S(2)}) copy-start(bf16[512,512]{1,0:T(8,128)(2,1)} %param.21) | copy-start | bytes 1572868
  206.4 16.9 %copy-start.8 = (f32[512]{0:T(512)S(1)}, f32[512]{0:T(512)}, u32[]{:S(2)}) copy-start(f32[512]{0:T(512)} %param.25) | copy-start | bytes 6148
  211.7 10.6 %all-to-all-start.1 = ((bf16[8,128,64]{1,2,0:T(8,128)(2,1)}), bf16[8,128,64]{1,2,0:T(8,128)(2,1)S(1)}, u32[]{:S(2)}, u32[]{:S(2)}) async-start(bf16[8,128,64]{1,2,0:T(8,128)(2,1)} %constant_dynamic-update-slice_fusion.3), calls=%async_computation.1 | async-start | bytes 262144 | tf_op jit(solution)/shard_map/all_to_all | solution.py:127
Sparse Core Ops, SparseCore 0:
  26.6 99.2 all-gather.1
